TPU v7x, 32 devices: a whole 2x2x4 slice. The times are simulated.
32 devices in a mesh: fsdp: 8 (over y, x, core), mode: 4 (over z).
Axes of the slice: x: 2, y: 2, z: 4, core: 2. Of those that a mesh axis runs over, the one named last changes fastest.
Arguments:
- gradient: float32 [32, 16, 2, 256, 512], P('mode', None, None, 'fsdp'), may hold values from -1000 to 1000, as said below
- start_in: float32 [512, 128], replicated, may hold values from -6 to 6
- start_out: float32 [256, 128], replicated, may hold values from -6 to 6
- start_x: float32 [32, 16], replicated, may hold values from -6 to 6
- start_y: float32 [16, 8], replicated, may hold values from -6 to 6
Outputs:
- factor_in: float32 [512, 128], P(('fsdp', 'mode'))
- factor_out: float32 [256, 128], P('fsdp')
- factor_x: float32 [32, 16], replicated
- factor_y: float32 [16, 8], replicated
- core: float32 [16, 128, 8, 2, 128], P('mode', 'fsdp')
Inputs may be any that keep to these rules, and one draw needn't show every extreme that they name: A weight gradient of one spectral layer, finite and bounded in magnitude.
All inputs are finite; a program needn't handle non-finite values.
Results may differ from a plain program's by a relative error of at most 0.0003.
Values sent between devices are 32-bit elements; how exact they have to be, the bound alone decides.
No kernel may reach another device: no remote copies, remote signals or barrier semaphores. Data moves between devices by JAX's collectives and lax.ppermute only.
A program may use at most 320 MiB of HBM per device.

v0:
```python
import jax
import jax.numpy as jnp
from jax import lax
from jax.sharding import PartitionSpec as P

I = 512
SWEEPS = 2
precise = lax.Precision.HIGHEST


def sweeps(gram, subspace):
    for sweep_index in range(SWEEPS):
        product = jnp.dot(gram, subspace, precision=precise)
        inner = jnp.dot(product.T, product, precision=precise)
        lower_factor = jnp.linalg.cholesky(inner)
        subspace = jax.scipy.linalg.solve_triangular(lower_factor, product.T, lower=True).T
    return subspace


def shards(gradient, start_in, start_out, start_x, start_y):
    fsdp_index = lax.axis_index("fsdp")
    mode_index = lax.axis_index("mode")
    joint_index = lax.axis_index(("fsdp", "mode"))
    fsdp_count = lax.axis_size("fsdp")
    mode_count = lax.axis_size("mode")
    rows_in = I // (fsdp_count * mode_count)
    local_first = gradient.shape[0]
    local_out = gradient.shape[3]
    gram_y_part = jnp.einsum("xycoi,xzcoi->yz", gradient, gradient, precision=precise)
    gram_in_part = jnp.einsum("xycoi,xycoj->ij", gradient, gradient, precision=precise)
    gram_in, gram_y = lax.psum((gram_in_part, gram_y_part), ("fsdp", "mode"))
    full_in = sweeps(gram_in, start_in)
    factor_y = sweeps(gram_y, start_y)
    by_out = lax.all_to_all(gradient, "fsdp", split_axis=4, concat_axis=3, tiled=True)
    gram_out = lax.psum(
        jnp.einsum("xycoi,xycpi->op", by_out, by_out, precision=precise), ("fsdp", "mode")
    )
    by_first = lax.all_to_all(gradient, "mode", split_axis=4, concat_axis=0, tiled=True)
    gram_x = lax.psum(
        jnp.einsum("xycoi,zycoi->xz", by_first, by_first, precision=precise), ("fsdp", "mode")
    )
    full_out = sweeps(gram_out, start_out)
    factor_x = sweeps(gram_x, start_x)
    partial_in = jnp.einsum("xycoi,ia->xycoa", gradient, full_in, precision=precise)
    out_rows = lax.dynamic_slice_in_dim(full_out, fsdp_index * local_out, local_out, 0)
    first_rows = lax.dynamic_slice_in_dim(factor_x, mode_index * local_first, local_first, 0)
    reduced = jnp.einsum("xycoa,yq->xqcoa", partial_in, factor_y, precision=precise)
    columns = first_rows
    partial_core = lax.psum_scatter(
        jnp.einsum("xqcoa,xp->pqcoa", reduced, columns, precision=precise),
        "mode",
        scatter_dimension=0,
        tiled=True,
    )
    columns = out_rows
    swapped = lax.psum_scatter(
        jnp.einsum("pqcoa,ob->bpqca", partial_core, columns, precision=precise),
        "fsdp",
        scatter_dimension=0,
        tiled=True,
    )
    core = jnp.transpose(swapped, (1, 0, 2, 3, 4))
    factor_in = lax.dynamic_slice_in_dim(full_in, joint_index * rows_in, rows_in, 0)
    return (factor_in, out_rows, factor_x, factor_y, core)


def solution(mesh):
    in_specs = (P("mode", None, None, "fsdp", None), P(), P(), P(), P())
    out_specs = (
        P(("fsdp", "mode"), None),
        P("fsdp", None),
        P(),
        P(),
        P("mode", "fsdp", None, None, None),
    )
    return jax.shard_map(shards, mesh=mesh, in_specs=in_specs, out_specs=out_specs, check_vma=False)
```

profile of v0, /device:TPU:0, one launch (start us, length us, event | category | flops | bytes accessed | tf_op | source)
XLA Modules:
  0.0 1270.9 jit_solution(15433066055648959006)
XLA Ops:
  7.2 50.4 %copy.78 = f32[8,16,2,32,512]{3,1,2,0,4:T(8,128)} copy(f32[8,16,2,32,512]{4,3,2,1,0:T(8,128)} %param.16) | data formatting | bytes 33554432 | tf_op args[0]
  57.6 67.0 %reshape.45 = f32[8,1,524288]{2,1,0:T(1,128)} reshape(f32[512,8,2,16,32]{4,3,2,1,0:T(8,128)} %bitcast.156) | data formatting | bytes 33554432
  124.6 5.7 all-to-all-start
  130.3 60.2 %reshape.47 = f32[4,1,1048576]{2,1,0:T(1,128)} reshape(f32[512,8,2,16,32]{4,3,2,1,0:T(8,128)} %bitcast.158) | data formatting | bytes 33554432
  190.5 124.4 %all-to-all-done = f32[8,1,524288]{2,1,0:T(1,128)} async-done(((f32[8,1,524288]{2,1,0:T(1,128)}), f32[8,1,524288]{2,1,0:T(1,128)}, u32[]{:S(2)}, u32[]{:S(2)}) %all-to-all-start) | async-done | bytes 16777248 | tf_op jit(solution)/shard_map/all_to_all | solution.py:34
  314.9 7.2 all-to-all-start.1
  322.2 31.6 %fusion.13 = f32[512,512]{1,0:T(8,128)} fusion(f32[8,16,2,32,512]{4,3,2,1,0:T(8,128)} %param.16), kind=kOutput, calls=%fused_computation.12 | convolution fusion | flops 25769803776 | bytes 17825792 | tf_op jit(solution)/shard_map/xycoi,xycoj->ij/dot_general | solution.py:30
  354.3 50.6 %reduce.12 = f32[8,524288]{1,0:T(8,128)} reduce(f32[8,1,524288]{2,1,0:T(1,128)} %all-to-all-done, f32[]{:T(128)} %broadcast.120), dimensions={1}, to_apply=%all_to_all.26.reduce_sub_computation | reduce | bytes 33554436 | tf_op jit(solution)/shard_map/all_to_all | solution.py:34
  404.9 55.4 %reshape.46 = f32[512,8,2,16,32]{4,3,2,1,0:T(8,128)} reshape(f32[8,524288]{1,0:T(8,128)} %reduce.12) | data formatting | bytes 33554432
  460.3 48.4 %copy.113 = f32[8,16,2,32,8,64]{5,3,4,1,0,2:T(8,128)} copy(f32[8,16,2,32,8,64]{3,1,2,0,5,4:T(8,128)} %bitcast.11) | data formatting | bytes 33554432 | tf_op jit(solution)/shard_map/all_to_all | solution.py:34
  508.7 36.8 %convolution_bitcast_fusion.1 = f32[256,256]{1,0:T(8,128)} fusion(f32[8,16,2,256,64]{4,3,1,0,2:T(8,128)} %bitcast.196), kind=kOutput, calls=%fused_computation.13 | convolution fusion | flops 12884901888 | bytes 17039360 | tf_op jit(solution)/shard_map/xycoi,xycpi->op/dot_general | solution.py:36
  545.6 51.9 %fusion.19 = f32[16,16]{1,0:T(8,128)S(1)} fusion(f32[8,16,2,32,512]{4,3,2,1,0:T(8,128)} %param.16), kind=kOutput, calls=%fused_computation.15 | convolution fusion | flops 805306368 | bytes 16778240 | tf_op jit(solution)/shard_map/xycoi,xzcoi->yz/dot_general | solution.py:29
  597.5 196.5 %all-reduce.4.cloned.1.call-done = (f32[512,512]{1,0:T(8,128)}, f32[256,256]{1,0:T(8,128)}) async-done(((f32[512,512]{1,0:T(8,128)}, f32[256,256]{1,0:T(8,128)}), (f32[512,512]{1,0:T(8,128)}, f32[256,256]{1,0:T(8,128)})) %all-reduce.4.cloned.1.call-update) | async-done | bytes 1310736 | tf_op jit(solution)/shard_map/psum | solution.py:31
  796.9 11.7 cholesky.158
  810.0 9.8 custom-call.22
  823.2 11.9 cholesky.169
  836.4 9.8 custom-call.23
  846.6 17.3 %convolution_bitcast_fusion = f32[8,16,2,32,128]{4,3,2,1,0:T(8,128)} fusion(f32[8,16,2,32,512]{4,3,2,1,0:T(8,128)} %param.16, f32[128,512]{1,0:T(8,128)S(1)} %fusion.23), kind=kOutput, calls=%fused_computation.8 | convolution fusion | flops 6442450944 | bytes 21233664 | tf_op jit(solution)/shard_map/xycoi,ia->xycoa/dot_general | solution.py:44
  864.0 54.5 %reduce.13 = f32[4,1048576]{1,0:T(4,128)} reduce(f32[4,1,1048576]{2,1,0:T(1,128)} %all-to-all-done.1, f32[]{:T(128)} %broadcast.120), dimensions={1}, to_apply=%all_to_all.30.reduce_sub_computation | reduce | bytes 33554436 | tf_op jit(solution)/shard_map/all_to_all | solution.py:38
  918.5 76.0 %reshape.48 = f32[512,8,2,16,32]{4,3,2,1,0:T(8,128)} reshape(f32[4,1048576]{1,0:T(4,128)} %reduce.13) | data formatting | bytes 33554432
  994.5 42.8 %copy.85 = f32[8,16,2,32,4,128]{5,0,4,1,3,2:T(8,128)} copy(f32[8,16,2,32,4,128]{3,1,2,0,5,4:T(8,128)} %bitcast.26) | data formatting | bytes 33554432 | tf_op jit(solution)/shard_map/all_to_all | solution.py:38
  1037.3 19.6 %fusion.16 = f32[32,32]{1,0:T(8,128)S(1)} fusion(f32[8,16,2,32,4,128]{5,0,4,1,3,2:T(8,128)} %copy.85), kind=kOutput, calls=%fused_computation.14 | convolution fusion | flops 1610612736 | bytes 16781312 | tf_op jit(solution)/shard_map/xycoi,zycoi->xz/dot_general | solution.py:40
  1057.0 39.5 %all-reduce = (f32[32,32]{1,0:T(8,128)S(1)}, f32[16,16]{1,0:T(8,128)S(1)}) all-reduce(f32[32,32]{1,0:T(8,128)S(1)} %fusion.16, f32[16,16]{1,0:T(8,128)S(1)} %fusion.19), channel_id=1, replica_groups=mesh['fsdp'=8,'mode'=4] {'fsdp','mode'}, use_global_device_ids=true, to_apply=%region_4.8 | all-reduce | flops 1280 | bytes 10240 | tf_op jit(solution)/shard_map/psum | solution.py:39
  1112.2 6.9 fusion.10
  1119.1 4.2 fusion.8
  1127.7 11.7 cholesky.180
  1140.8 9.8 custom-call.24
  1151.8 11.7 cholesky.191
  1164.9 10.0 custom-call.25
  1175.2 28.3 %reduce-scatter.3.cloned.1.call-done = f32[4,8,2,32,128]{4,3,2,1,0:T(8,128)} async-done(((f32[16,8,2,32,128]{4,3,2,1,0:T(8,128)}), f32[4,8,2,32,128]{4,3,2,1,0:T(8,128)}) %reduce-scatter.3.cloned.1.call-update) | async-done | bytes 1048592 | tf_op jit(solution)/shard_map/reduce_scatter | solution.py:49
  1203.4 6.6 fusion.45
  1211.5 50.3 %reduce-scatter.5.cloned.1.call-done = f32[16,4,8,2,128]{4,0,3,2,1:T(8,128)} async-done(((f32[128,4,8,2,128]{4,0,3,2,1:T(8,128)}), f32[16,4,8,2,128]{4,0,3,2,1:T(8,128)}) %reduce-scatter.5.cloned.1.call-update) | async-done | bytes 524304 | tf_op jit(solution)/shard_map/reduce_scatter | solution.py:56
  (99 shorter events, 37.5 us)
Async XLA Ops:
  7.2 786.8 %copy-start = (f32[512,128]{1,0:T(8,128)S(1)}, f32[512,128]{1,0:T(8,128)}, u32[]{:S(2)}) copy-start(f32[512,128]{1,0:T(8,128)} %param.17) | copy-start | bytes 786436
  124.6 190.3 %all-to-all-start = ((f32[8,1,524288]{2,1,0:T(1,128)}), f32[8,1,524288]{2,1,0:T(1,128)}, u32[]{:S(2)}, u32[]{:S(2)}) async-start(f32[8,1,524288]{2,1,0:T(1,128)} %reshape.45), calls=%async_computation | async-start | bytes 33554432 | tf_op jit(solution)/shard_map/all_to_all | solution.py:34
  314.9 549.1 %all-to-all-start.1 = ((f32[4,1,1048576]{2,1,0:T(1,128)}), f32[4,1,1048576]{2,1,0:T(1,128)}, u32[]{:S(2)}, u32[]{:S(2)}) async-start(f32[4,1,1048576]{2,1,0:T(1,128)} %reshape.47), calls=%async_computation.1 | async-start | bytes 33554432 | tf_op jit(solution)/shard_map/all_to_all | solution.py:38
  322.1 471.9 %all-reduce.4.cloned.1.call-start = ((), (), s32[]{:S(2)}) async-start(), calls=%async_computation.6 | async-start | bytes 2621440 | tf_op jit(solution)/shard_map/psum | solution.py:31
  545.5 657.9 %reduce-scatter.3.cloned.1.call-start = ((), (), s32[]{:S(2)}) async-start(), calls=%async_computation.4 | async-start | bytes 5242880 | tf_op jit(solution)/shard_map/reduce_scatter | solution.py:49
  1037.3 59.2 %copy-start.6 = (f32[16,8]{0,1:T(8,128)S(1)}, f32[16,8]{0,1:T(8,128)}, u32[]{:S(2)}) copy-start(f32[16,8]{0,1:T(8,128)} %param.20) | copy-start | bytes 1540
  1037.3 65.7 %copy-start.5 = (f32[32,16]{0,1:T(8,128)S(1)}, f32[32,16]{0,1:T(8,128)}, u32[]{:S(2)}) copy-start(f32[32,16]{0,1:T(8,128)} %param.19) | copy-start | bytes 6148
  1056.9 69.9 %copy-start.1 = (f32[256,256]{1,0:T(8,128)S(1)}, f32[256,256]{1,0:T(8,128)}, u32[]{:S(2)}) copy-start(f32[256,256]{1,0:T(8,128)} %get-tuple-element.35) | copy-start | bytes 786436
  1057.0 69.9 %copy-start.2 = (f32[256,128]{1,0:T(8,128)S(1)}, f32[256,128]{1,0:T(8,128)}, u32[]{:S(2)}) copy-start(f32[256,128]{1,0:T(8,128)} %param.18) | copy-start | bytes 393220
  1103.0 107.1 %copy-start.4 = (f32[8,16]{1,0:T(8,128)}, f32[8,16]{1,0:T(8,128)S(1)}, u32[]{:S(2)}) copy-start(f32[8,16]{1,0:T(8,128)S(1)} %fusion.64) | copy-start | bytes 1540
  1112.2 97.9 %copy-start.3 = (f32[16,32]{1,0:T(8,128)}, f32[16,32]{1,0:T(8,128)S(1)}, u32[]{:S(2)}) copy-start(f32[16,32]{1,0:T(8,128)S(1)} %fusion.51) | copy-start | bytes 6148
  1126.5 135.2 %reduce-scatter.5.cloned.1.call-start = ((), (), s32[]{:S(2)}) async-start(), calls=%async_computation.5 | async-start | bytes 4718592 | tf_op jit(solution)/shard_map/reduce_scatter | solution.py:56
Sparse Core Ops, SparseCore 0:
  545.6 248.3 all-reduce.3
  1126.7 76.7 reduce-scatter.2
  1210.2 51.5 reduce-scatter.4
where the time goes:
time: 1280 us; the launch traced here: 1270 us
  local copies, waits for them, and re-layouts  408 us (32%)
  waiting for transfers between devices  400 us (31%)
  other arithmetic  210 us (16%)
  matrix products  185 us (14%)
  blocking collectives  39.5 us (3%)
  between operations  14.6 us (1%)
  starting transfers between devices  13.3 us (1%)
    unnamed x21, local copies, waits for them, and re-layouts  312 us
    psum x1, waiting for transfers between devices, shards(): gram_in, gram_y = lax.psum((gram_in_part, gram_y_part), ('fsdp', 'mode'))  197 us
    all_to_all x1, waiting for transfers between devices, shards(): lax.all_to_all(gradient, 'fsdp', split_axis=4, concat_axis=3, tiled=True)  124 us
    another operation x24, other arithmetic, sweeps(): lower_factor = jnp.linalg.cholesky(inner)  56.9 us
    all_to_all x1, other arithmetic, shards(): lax.all_to_all(gradient, 'mode', split_axis=4, concat_axis=0, tiled=True)  54.5 us
    dot_general x1, matrix products, shards(): jnp.einsum('xycoi,xzcoi->yz', gradient, gradient, precision=precise)  51.9 us
    all_to_all x1, other arithmetic, shards(): lax.all_to_all(gradient, 'fsdp', split_axis=4, concat_axis=3, tiled=True)  50.6 us
    reduce_scatter x1, waiting for transfers between devices, shards(): lax.psum_scatter(jnp.einsum('pqcoa,ob->bpqca', partial_core, columns, pre...  50.3 us
  transfers between devices with their start and end apart: 5, of which 4 were waited for; matrix products, arithmetic and copies ran while one was open for 36% of the time, Pallas kernels for 0%

commit v1 on v0

--- a/solution.py
+++ b/solution.py
@@ -28,7 +28,7 @@
     local_out = gradient.shape[3]
     gram_y_part = jnp.einsum("xycoi,xzcoi->yz", gradient, gradient, precision=precise)
     gram_in_part = jnp.einsum("xycoi,xycoj->ij", gradient, gradient, precision=precise)
-    gram_in, gram_y = lax.psum((gram_in_part, gram_y_part), ("fsdp", "mode"))
+    gram_in, gram_y = lax.psum(lax.psum((gram_in_part, gram_y_part), "mode"), "fsdp")
     full_in = sweeps(gram_in, start_in)
     factor_y = sweeps(gram_y, start_y)
     by_out = lax.all_to_all(gradient, "fsdp", split_axis=4, concat_axis=3, tiled=True)

time: 1280 us -> 1460 us (1.14)
  blocking collectives: 39.5 us -> 276 us
  waiting for transfers between devices: 400 us -> 344 us
    psum x0 -> x2, blocking collectives: none -> 237 us  [the longest x1 223 us: shards(): lax.psum((gram_in_part, gram_y_part), 'mode')]
    psum x1 -> x3, waiting for transfers between devices: 197 us -> 143 us  [the longest x1 143 us: shards(): lax.psum(lax.psum((gram_in_part, gram_y_part), 'mode'), 'fsdp')]
    unnamed x21 -> x23, local copies, waits for them, and re-layouts: 312 us -> 313 us
  transfers between devices with their start and end apart: 5 -> 7, of which waited for: 4 -> 4; matrix products, arithmetic and copies ran while one was open for 36% -> 47% of each run, Pallas kernels for 0% -> 0%
where the time goes in v1:
time: 1460 us; the launch traced here: 1450 us
  local copies, waits for them, and re-layouts  410 us (28%)
  waiting for transfers between devices  344 us (24%)
  blocking collectives  276 us (19%)
  other arithmetic  210 us (14%)
  matrix products  184 us (13%)
  between operations  16.1 us (1%)
    unnamed x23, local copies, waits for them, and re-layouts  313 us
    psum x1, blocking collectives, shards(): lax.psum((gram_in_part, gram_y_part), 'mode')  223 us
    psum x1, waiting for transfers between devices, shards(): lax.psum(lax.psum((gram_in_part, gram_y_part), 'mode'), 'fsdp')  143 us
    all_to_all x1, waiting for transfers between devices, shards(): lax.all_to_all(gradient, 'fsdp', split_axis=4, concat_axis=3, tiled=True)  124 us
    another operation x24, other arithmetic, sweeps(): lower_factor = jnp.linalg.cholesky(inner)  57 us
    all_to_all x1, other arithmetic, shards(): lax.all_to_all(gradient, 'mode', split_axis=4, concat_axis=0, tiled=True)  54.2 us
    dot_general x1, matrix products, shards(): jnp.einsum('xycoi,xzcoi->yz', gradient, gradient, precision=precise)  51.8 us
    all_to_all x1, other arithmetic, shards(): lax.all_to_all(gradient, 'fsdp', split_axis=4, concat_axis=3, tiled=True)  50.2 us
  transfers between devices with their start and end apart: 7, of which 4 were waited for; matrix products, arithmetic and copies ran while one was open for 47% of the time, Pallas kernels for 0%

profile of v1, /device:TPU:0, one launch (start us, length us, event | category | flops | bytes accessed | tf_op | source)
XLA Modules:
  0.0 1453.4 jit_solution(9082057743548179306)
XLA Ops:
  8.0 50.4 %copy.78 = f32[8,16,2,32,512]{3,1,2,0,4:T(8,128)} copy(f32[8,16,2,32,512]{4,3,2,1,0:T(8,128)} %param.16) | data formatting | bytes 33554432 | tf_op args[0]
  58.4 67.0 %reshape.45 = f32[8,1,524288]{2,1,0:T(1,128)} reshape(f32[512,8,2,16,32]{4,3,2,1,0:T(8,128)} %bitcast.156) | data formatting | bytes 33554432
  125.4 5.7 all-to-all-start
  131.2 60.2 %reshape.47 = f32[4,1,1048576]{2,1,0:T(1,128)} reshape(f32[512,8,2,16,32]{4,3,2,1,0:T(8,128)} %bitcast.158) | data formatting | bytes 33554432
  191.3 124.4 %all-to-all-done = f32[8,1,524288]{2,1,0:T(1,128)} async-done(((f32[8,1,524288]{2,1,0:T(1,128)}), f32[8,1,524288]{2,1,0:T(1,128)}, u32[]{:S(2)}, u32[]{:S(2)}) %all-to-all-start) | async-done | bytes 16777248 | tf_op jit(solution)/shard_map/all_to_all | solution.py:34
  315.8 7.2 all-to-all-start.1
  323.0 31.6 %fusion.13 = f32[512,512]{1,0:T(8,128)} fusion(f32[8,16,2,32,512]{4,3,2,1,0:T(8,128)} %param.16), kind=kOutput, calls=%fused_computation.12 | convolution fusion | flops 25769803776 | bytes 17825792 | tf_op jit(solution)/shard_map/xycoi,xycoj->ij/dot_general | solution.py:30
  355.1 51.8 %fusion.19 = f32[16,16]{1,0:T(8,128)S(1)} fusion(f32[8,16,2,32,512]{4,3,2,1,0:T(8,128)} %param.16), kind=kOutput, calls=%fused_computation.15 | convolution fusion | flops 805306368 | bytes 16778240 | tf_op jit(solution)/shard_map/xycoi,xzcoi->yz/dot_general | solution.py:29
  406.9 222.9 %psum.46 = f32[16,16]{1,0:T(8,128)S(1)} all-reduce(f32[16,16]{1,0:T(8,128)S(1)} %fusion.19), channel_id=1, replica_groups=mesh['fsdp'=8,'mode'=4] {'mode'}, use_global_device_ids=true, to_apply=%region_8.14 | all-reduce | flops 256 | bytes 2048 | tf_op jit(solution)/shard_map/psum | solution.py:31
  629.7 13.8 psum.47
  650.3 143.1 %all-reduce.6.cloned.1.call-done = f32[512,512]{1,0:T(8,128)} async-done(((f32[512,512]{1,0:T(8,128)}), f32[512,512]{1,0:T(8,128)}) %all-reduce.6.cloned.1.call-update) | async-done | bytes 1048592 | tf_op jit(solution)/shard_map/psum | solution.py:31
  796.3 11.7 cholesky.158
  809.4 9.8 custom-call.22
  822.5 12.1 cholesky.169
  836.0 9.8 custom-call.23
  846.9 16.6 %convolution_bitcast_fusion = f32[8,16,2,32,128]{4,3,2,1,0:T(8,128)S(1)} fusion(f32[8,16,2,32,512]{4,3,2,1,0:T(8,128)} %param.16, f32[128,512]{1,0:T(8,128)S(1)} %fusion.23), kind=kOutput, calls=%fused_computation.8 | convolution fusion | flops 6442450944 | bytes 21233664 | tf_op jit(solution)/shard_map/xycoi,ia->xycoa/dot_general | solution.py:44
  868.4 50.2 %reduce.12 = f32[8,524288]{1,0:T(8,128)} reduce(f32[8,1,524288]{2,1,0:T(1,128)} %all-to-all-done, f32[]{:T(128)} %broadcast.120), dimensions={1}, to_apply=%all_to_all.26.reduce_sub_computation | reduce | bytes 33554436 | tf_op jit(solution)/shard_map/all_to_all | solution.py:34
  918.6 55.4 %reshape.46 = f32[512,8,2,16,32]{4,3,2,1,0:T(8,128)} reshape(f32[8,524288]{1,0:T(8,128)} %reduce.12) | data formatting | bytes 33554432
  974.1 48.4 %copy.113 = f32[8,16,2,32,8,64]{5,3,4,1,0,2:T(8,128)} copy(f32[8,16,2,32,8,64]{3,1,2,0,5,4:T(8,128)} %bitcast.11) | data formatting | bytes 33554432 | tf_op jit(solution)/shard_map/all_to_all | solution.py:34
  1022.5 36.8 %convolution_bitcast_fusion.1 = f32[256,256]{1,0:T(8,128)} fusion(f32[8,16,2,256,64]{4,3,1,0,2:T(8,128)} %bitcast.196), kind=kOutput, calls=%fused_computation.13 | convolution fusion | flops 12884901888 | bytes 17039360 | tf_op jit(solution)/shard_map/xycoi,xycpi->op/dot_general | solution.py:36
  1059.3 54.2 %reduce.13 = f32[4,1048576]{1,0:T(4,128)} reduce(f32[4,1,1048576]{2,1,0:T(1,128)} %all-to-all-done.1, f32[]{:T(128)} %broadcast.120), dimensions={1}, to_apply=%all_to_all.30.reduce_sub_computation | reduce | bytes 33554436 | tf_op jit(solution)/shard_map/all_to_all | solution.py:38
  1113.5 76.3 %reshape.48 = f32[512,8,2,16,32]{4,3,2,1,0:T(8,128)} reshape(f32[4,1048576]{1,0:T(4,128)} %reduce.13) | data formatting | bytes 33554432
  1189.9 42.8 %copy.85 = f32[8,16,2,32,4,128]{5,0,4,1,3,2:T(8,128)} copy(f32[8,16,2,32,4,128]{3,1,2,0,5,4:T(8,128)} %bitcast.26) | data formatting | bytes 33554432 | tf_op jit(solution)/shard_map/all_to_all | solution.py:38
  1232.7 19.6 %fusion.16 = f32[32,32]{1,0:T(8,128)S(1)} fusion(f32[8,16,2,32,4,128]{5,0,4,1,3,2:T(8,128)} %copy.85), kind=kOutput, calls=%fused_computation.14 | convolution fusion | flops 1610612736 | bytes 16781312 | tf_op jit(solution)/shard_map/xycoi,zycoi->xz/dot_general | solution.py:40
  1252.3 39.4 %psum.45 = f32[32,32]{1,0:T(8,128)S(1)} all-reduce(f32[32,32]{1,0:T(8,128)S(1)} %fusion.16), channel_id=1, replica_groups=mesh['fsdp'=8,'mode'=4] {'fsdp','mode'}, use_global_device_ids=true, to_apply=%region_5.9 | all-reduce | flops 1024 | bytes 8192 | tf_op jit(solution)/shard_map/psum | solution.py:39
  1310.5 11.7 cholesky.180
  1323.6 9.8 custom-call.24
  1335.6 11.7 cholesky.191
  1348.6 10.0 custom-call.25
  1358.9 26.3 %reduce-scatter.3.cloned.1.call-done = f32[4,8,2,32,128]{4,3,2,1,0:T(8,128)} async-done(((f32[16,8,2,32,128]{4,3,2,1,0:T(8,128)}), f32[4,8,2,32,128]{4,3,2,1,0:T(8,128)}) %reduce-scatter.3.cloned.1.call-update) | async-done | bytes 1048592 | tf_op jit(solution)/shard_map/reduce_scatter | solution.py:49
  1385.3 6.7 fusion.45
  1394.2 49.6 %reduce-scatter.5.cloned.1.call-done = f32[16,4,8,2,128]{4,0,3,2,1:T(8,128)} async-done(((f32[128,4,8,2,128]{4,0,3,2,1:T(8,128)}), f32[16,4,8,2,128]{4,0,3,2,1:T(8,128)}) %reduce-scatter.5.cloned.1.call-update) | async-done | bytes 524304 | tf_op jit(solution)/shard_map/reduce_scatter | solution.py:56
  (109 shorter events, 50.4 us)
Async XLA Ops:
  8.0 785.4 %copy-start = (f32[512,128]{1,0:T(8,128)S(1)}, f32[512,128]{1,0:T(8,128)}, u32[]{:S(2)}) copy-start(f32[512,128]{1,0:T(8,128)} %param.17) | copy-start | bytes 786436
  125.4 190.4 %all-to-all-start = ((f32[8,1,524288]{2,1,0:T(1,128)}), f32[8,1,524288]{2,1,0:T(1,128)}, u32[]{:S(2)}, u32[]{:S(2)}) async-start(f32[8,1,524288]{2,1,0:T(1,128)} %reshape.45), calls=%async_computation | async-start | bytes 33554432 | tf_op jit(solution)/shard_map/all_to_all | solution.py:34
  315.8 743.6 %all-to-all-start.1 = ((f32[4,1,1048576]{2,1,0:T(1,128)}), f32[4,1,1048576]{2,1,0:T(1,128)}, u32[]{:S(2)}, u32[]{:S(2)}) async-start(f32[4,1,1048576]{2,1,0:T(1,128)} %reshape.47), calls=%async_computation.1 | async-start | bytes 33554432 | tf_op jit(solution)/shard_map/all_to_all | solution.py:38
  323.0 324.9 %all-reduce.4.cloned.1.call-start = ((), (), s32[]{:S(2)}) async-start(), calls=%async_computation.4 | async-start | bytes 2097152 | tf_op jit(solution)/shard_map/psum | solution.py:31
  354.6 288.9 %copy-start.7 = (f32[16,8]{0,1:T(8,128)S(1)}, f32[16,8]{0,1:T(8,128)}, u32[]{:S(2)}) copy-start(f32[16,8]{0,1:T(8,128)} %param.20) | copy-start | bytes 1540
  354.7 438.7 %all-reduce.6.cloned.1.call-start = ((), (), s32[]{:S(2)}) async-start(), calls=%async_computation.5 | async-start | bytes 2097152 | tf_op jit(solution)/shard_map/psum | solution.py:31
  647.9 660.8 %all-reduce.8.cloned.1.call-start = ((), (), s32[]{:S(2)}) async-start(), calls=%async_computation.6 | async-start | bytes 524288 | tf_op jit(solution)/shard_map/psum | solution.py:35
  650.3 217.6 %copy-start.5 = (f32[8,16]{1,0:T(8,128)}, f32[8,16]{1,0:T(8,128)S(1)}, u32[]{:S(2)}) copy-start(f32[8,16]{1,0:T(8,128)S(1)} %fusion.64) | copy-start | bytes 1540
  846.2 0.7 copy-start.2
  1059.3 326.0 %reduce-scatter.3.cloned.1.call-start = ((), (), s32[]{:S(2)}) async-start(), calls=%async_computation.7 | async-start | bytes 5242880 | tf_op jit(solution)/shard_map/reduce_scatter | solution.py:49
  1232.7 59.0 %copy-start.6 = (f32[32,16]{0,1:T(8,128)S(1)}, f32[32,16]{0,1:T(8,128)}, u32[]{:S(2)}) copy-start(f32[32,16]{0,1:T(8,128)} %param.19) | copy-start | bytes 6148
  1232.7 76.0 %copy-start.3 = (f32[256,128]{1,0:T(8,128)S(1)}, f32[256,128]{1,0:T(8,128)}, u32[]{:S(2)}) copy-start(f32[256,128]{1,0:T(8,128)} %param.18) | copy-start | bytes 393220
  1232.7 213.2 %copy-start.1 = (f32[512,128]{1,0:T(8,128)S(1)}, f32[512,128]{1,0:T(8,128)}, u32[]{:S(2)}) copy-start(f32[512,128]{1,0:T(8,128)} %param.17) | copy-start | bytes 786436
  1300.8 145.0 %copy-start.4 = (f32[16,32]{1,0:T(8,128)}, f32[16,32]{1,0:T(8,128)S(1)}, u32[]{:S(2)}) copy-start(f32[16,32]{1,0:T(8,128)S(1)} %fusion.51) | copy-start | bytes 6148
  1308.4 135.4 %reduce-scatter.5.cloned.1.call-start = ((), (), s32[]{:S(2)}) async-start(), calls=%async_computation.8 | async-start | bytes 4718592 | tf_op jit(solution)/shard_map/reduce_scatter | solution.py:56
Sparse Core Ops, SparseCore 0:
  354.8 128.8 all-reduce.3
  648.0 145.2 all-reduce.5
  1308.5 76.7 reduce-scatter.2
  1392.1 51.6 reduce-scatter.4
Sparse Core Ops, SparseCore 1:
  1059.4 125.2 all-reduce.7
